TPU v7x, 32 devices: a whole 2x2x4 slice. The times are simulated.
32 devices in a mesh: dom: 16 (over z, x, core), band: 2 (over y).
Axes of the slice: x: 2, y: 2, z: 4, core: 2. Of those that a mesh axis runs over, the one named last changes fastest.
Arguments:
- wavefun: float32 [13824, 512], P('dom', 'band')
- cell_ops: float32 [64, 343, 343], P('dom'), as said below
- cell_map: int32 [64, 343], P('dom'), may hold values from 0 to 1007, as said below
- face_list: int32 [2304], P('dom'), may hold values from 0 to 863, as said below
Outputs:
- ortho_bands: float32 [13824, 512], P('dom', 'band')
Inputs may be any that keep to these rules, and one draw needn't show every extreme that they name: `cell_map`: each row lists the 343 distinct local numbers of a cell's nodes; a number below 864 is a node of the cell's own domain, 864 + j stands for the j-th lower face node of the next domain (periodic over domains); every node of a domain belongs to some cell of that domain. `face_list`: the 144 entries of each domain are distinct node numbers of that domain. `cell_ops`: each cell's matrix is symmetric.
All inputs are finite; a program needn't handle non-finite values.
Results may differ from a plain program's by a relative error of at most 0.0001.
Values sent between devices are 32-bit elements; how exact they have to be, the bound alone decides.
A program may use at most 64 MiB of HBM per device.

v0:
```python
import jax
import jax.numpy as jnp
from jax import lax
from jax.sharding import PartitionSpec as P

DEGREE = 2


cheb_centre = 1.0
cheb_half = 1.6


def shifted(block, axis, distance):
    devices = range(lax.axis_size(axis))
    route = [((i - distance) % len(devices), i) for i in devices]
    return lax.ppermute(block, axis, route)


def on_device(wavefun, cell_ops, cell_map, face_list):
    owned_rows = wavefun.shape[0]
    block_width = wavefun.shape[1]
    flat_map = cell_map.reshape(-1)

    def local_apply(extended):
        cell_values = extended[flat_map].reshape(cell_map.shape[0], cell_map.shape[1], block_width)
        products = jnp.einsum(
            "cij,cjb->cib", cell_ops, cell_values, precision=lax.Precision.HIGHEST
        )
        return jnp.zeros_like(extended).at[flat_map].add(products.reshape(-1, block_width))

    def operate(vector):
        fetched = shifted(vector[face_list], "dom", -1)
        applied = local_apply(jnp.concatenate([vector, fetched], 0))
        returned = shifted(applied[owned_rows:], "dom", 1)
        return applied[:owned_rows].at[face_list].add(returned)

    latest = (operate(wavefun) - cheb_centre * wavefun) / cheb_half

    def advance(counter, carried):
        earlier, current = carried
        following = 2.0 * (operate(current) - cheb_centre * current) / cheb_half - earlier
        return (current, following)

    earlier, latest = lax.fori_loop(1, DEGREE, advance, (wavefun, latest))
    full_bands = lax.all_gather(latest, "band", axis=1, tiled=True)
    partial_value = jnp.einsum("nb,nc->bc", full_bands, full_bands, precision=lax.Precision.HIGHEST)
    margin = lax.psum(partial_value, "dom")
    norm_value = jnp.sqrt(jnp.sum(margin * margin) + 1e-06)
    full_width = margin.shape[0]
    offset = lax.axis_index("band") * block_width
    scaled_cols = lax.dynamic_slice_in_dim(margin, offset, block_width, 1) / norm_value
    identity_cols = lax.dynamic_slice_in_dim(
        jnp.eye(full_width, dtype=jnp.float32), offset, block_width, 1
    )
    mixing = (3.0 * identity_cols - scaled_cols) / 2.0
    return jnp.dot(full_bands, mixing, precision=lax.Precision.HIGHEST)


def solution(mesh):
    return jax.shard_map(
        on_device,
        mesh=mesh,
        in_specs=(P("dom", "band"), P("dom", None, None), P("dom", None), P("dom")),
        out_specs=P("dom", "band"),
        check_vma=False,
    )
```

profile of v0, /device:TPU:0, one launch (start us, length us, event | category | flops | bytes accessed | tf_op | source)
XLA Modules:
  0.0 234.2 jit_solution(618638592340945098)
XLA Ops:
  6.5 0.8 compare_select_fusion.1
  7.4 2.0 gather_fusion
  9.3 5.5 %collective-permute-start = (f32[144,256]{1,0:T(8,128)S(1)}, f32[144,256]{1,0:T(8,128)S(1)}, u32[]{:S(2)}, u32[]{:S(2)}) collective-permute-start(f32[144,256]{1,0:T(8,128)S(1)} %gather_fusion), channel_id=1, source_target_pairs={{2,0},{4,2},{6,4},{8,6},{10,8},{12,10},{14,12},{16,14},{18,16},{20... | collective-permute-start | bytes 442376 | tf_op jit(solution)/shard_map/ppermute | solution.py:16
  15.7 1.9 collective-permute-done
  17.5 1.2 pad_maximum_fusion
  18.7 4.6 %gather_fusion.1 = f32[1372,256]{1,0:T(8,128)} fusion(f32[1008,256]{1,0:T(8,128)S(1)} %pad_maximum_fusion, s32[2048]{0:T(1024)S(1)} %pad_clamp_fusion), kind=kCustom, calls=%fused_computation.1 | custom fusion | bytes 2815344 | tf_op jit(solution)/shard_map/gather | solution.py:25
  23.3 1.5 reshape.46
  24.8 3.7 %fusion.4 = f32[4,343,256]{2,1,0:T(8,128)} fusion(f32[4,343,256]{2,1,0:T(8,128)S(1)} %reshape.46, f32[4,343,343]{2,0,1:T(4,128)S(1)} %copy-done), kind=kOutput, calls=%fused_computation.12 | convolution fusion | flops 1445670912 | bytes 4692240 | tf_op jit(solution)/shard_map/cij,cjb->cib/dot_general | solution.py:26
  28.5 2.6 %reshape.86 = f32[1372,256]{1,0:T(8,128)} reshape(f32[4,343,256]{2,1,0:T(8,128)} %fusion.4) | data formatting | bytes 2809856 | tf_op jit(solution)/shard_map/reshape | solution.py:29
  31.1 8.7 %scatter_custom_fusion = f32[1008,256]{1,0:T(8,128)S(1)} fusion(s32[1372]{0:T(1024)S(1)} %fusion.25, f32[1372,256]{1,0:T(8,128)} %reshape.86, f32[]{:T(128)} %constant.12.clone.1), kind=kCustom, calls=%fused_computation.29 | custom fusion | flops 351232 | bytes 1032704 | tf_op jit(solution)/shard_map/scatter-add | solution.py:29
  39.9 1.0 copy-done.3
  40.9 1.2 slice.26
  42.1 6.2 %collective-permute-done.1 = f32[144,256]{1,0:T(8,128)S(1)} collective-permute-done((f32[144,256]{1,0:T(8,128)S(1)}, f32[144,256]{1,0:T(8,128)S(1)}, u32[]{:S(2)}, u32[]{:S(2)}) %collective-permute-start.1) | collective-permute-done | bytes 147488 | tf_op jit(solution)/shard_map/ppermute | solution.py:16
  48.3 1.7 scatter_fusion
  50.0 2.6 %subtract_multiply_fusion = f32[864,256]{1,0:T(8,128)} fusion(f32[864,256]{1,0:T(8,128)S(1)} %scatter_fusion, f32[864,256]{1,0:T(8,128)} %param.4), kind=kLoop, calls=%fused_computation.18 | loop fusion | flops 442368 | bytes 2654208 | tf_op jit(solution)/shard_map/div | solution.py:37
  52.5 2.0 gather_fusion.2
  54.8 2.7 %collective-permute-done.2 = f32[144,256]{1,0:T(8,128)S(1)} collective-permute-done((f32[144,256]{1,0:T(8,128)S(1)}, f32[144,256]{1,0:T(8,128)S(1)}, u32[]{:S(2)}, u32[]{:S(2)}) %collective-permute-start.2) | collective-permute-done | bytes 147488 | tf_op jit(solution)/shard_map/while/body/eval_jaxpr/ppermute | solution.py:16
  57.4 1.2 pad_maximum_fusion.1
  58.7 4.6 %gather_fusion.3 = f32[1372,256]{1,0:T(8,128)} fusion(f32[1008,256]{1,0:T(8,128)S(1)} %pad_maximum_fusion.1, s32[2048]{0:T(1024)S(1)} %pad_clamp_fusion), kind=kCustom, calls=%fused_computation.3 | custom fusion | bytes 2815344 | tf_op jit(solution)/shard_map/while/body/eval_jaxpr/gather | solution.py:25
  63.2 1.5 reshape.48
  64.7 3.7 %fusion.7 = f32[4,343,256]{2,1,0:T(8,128)} fusion(f32[4,343,256]{2,1,0:T(8,128)S(1)} %reshape.48, f32[4,343,343]{2,0,1:T(4,128)S(1)} %copy-done), kind=kOutput, calls=%fused_computation.13 | convolution fusion | flops 1445670912 | bytes 4692240 | tf_op jit(solution)/shard_map/while/body/eval_jaxpr/cij,cjb->cib/dot_general | solution.py:26
  68.4 2.6 %reshape.102 = f32[1372,256]{1,0:T(8,128)} reshape(f32[4,343,256]{2,1,0:T(8,128)} %fusion.7) | data formatting | bytes 2809856 | tf_op jit(solution)/shard_map/while/body/eval_jaxpr/reshape | solution.py:29
  71.0 8.7 %scatter_custom_fusion.2 = f32[1008,256]{1,0:T(8,128)S(1)} fusion(s32[1372]{0:T(1024)S(1)} %fusion.25, f32[1372,256]{1,0:T(8,128)} %reshape.102, f32[]{:T(128)} %constant.12.clone.1), kind=kCustom, calls=%fused_computation.27 | custom fusion | flops 351232 | bytes 1032704 | tf_op jit(solution)/shard_map/while/body/eval_jaxpr/scatter-add | solution.py:29
  79.8 1.0 slice.28
  80.8 6.4 %collective-permute-done.3 = f32[144,256]{1,0:T(8,128)S(1)} collective-permute-done((f32[144,256]{1,0:T(8,128)S(1)}, f32[144,256]{1,0:T(8,128)S(1)}, u32[]{:S(2)}, u32[]{:S(2)}) %collective-permute-start.3) | collective-permute-done | bytes 147488 | tf_op jit(solution)/shard_map/while/body/eval_jaxpr/ppermute | solution.py:16
  87.3 3.3 %scatter_fusion.1 = f32[864,256]{1,0:T(8,128)} fusion(f32[864,256]{1,0:T(8,128)} %slice.28, s32[144]{0:T(256)S(1)} %compare_select_fusion.1, f32[144,256]{1,0:T(8,128)S(1)} %collective-permute-done.3), kind=kCustom, calls=%fused_computation.7 | custom fusion | flops 36864 | bytes 442944 | tf_op jit(solution)/shard_map/while/body/eval_jaxpr/scatter-add | solution.py:35
  90.6 2.6 %multiply_subtract_fusion = f32[864,256]{1,0:T(8,128)} fusion(f32[864,256]{1,0:T(8,128)} %param.4, f32[864,256]{1,0:T(8,128)} %scatter_fusion.1, f32[864,256]{1,0:T(8,128)S(1)} %copy-done.2), kind=kLoop, calls=%fused_computation.17 | loop fusion | flops 1105920 | bytes 3538944 | tf_op jit(solution)/shard_map/while/body/eval_jaxpr/sub | solution.py:41
  93.5 26.6 %all-gather.2.cloned.1.call-done = f32[864,512]{1,0:T(8,128)} async-done(((f32[864,256]{1,0:T(8,128)}), f32[864,512]{1,0:T(8,128)}) %all-gather.2.cloned.1.call-update) | async-done | bytes 1769488 | tf_op jit(solution)/shard_map/all_gather | solution.py:45
  120.0 6.5 %fusion.29 = f32[512,512]{1,0:T(8,128)} fusion(f32[864,512]{1,0:T(8,128)} %all-gather.2.cloned.1.call-done), kind=kOutput, calls=%fused_computation.43 | convolution fusion | flops 2717908992 | bytes 2818048 | tf_op jit(solution)/shard_map/nb,nc->bc/dot_general | solution.py:46
  126.6 93.8 %all-reduce.2.cloned.1.call-done = f32[512,512]{1,0:T(8,128)} async-done(((f32[512,512]{1,0:T(8,128)}), f32[512,512]{1,0:T(8,128)}) %all-reduce.2.cloned.1.call-update) | async-done | bytes 1048592 | tf_op jit(solution)/shard_map/psum | solution.py:47
  220.5 2.1 multiply_reduce_fusion
  223.2 4.1 %fusion.10 = f32[864,256]{1,0:T(8,128)} fusion(f32[864,512]{1,0:T(8,128)} %all-gather.2.cloned.1.call-done, f32[512,512]{1,0:T(8,128)} %all-reduce.2.cloned.1.call-done, s32[]{:T(128)S(6)} %select_n.27, f32[]{:T(128)S(6)} %sqrt.3), kind=kOutput, calls=%fused_computation.20 | convolution fusion | flops 1359872000 | bytes 3180032 | tf_op jit(solution)/shard_map/dot_general | solution.py:56
  (20 shorter events, 1.4 us)
Async XLA Ops:
  6.5 18.3 %copy-start = (f32[4,343,343]{2,0,1:T(4,128)S(1)}, f32[4,343,343]{2,0,1:T(4,128)}, u32[]{:S(2)}) copy-start(f32[4,343,343]{2,0,1:T(4,128)} %param.5) | copy-start | bytes 5647156
  6.5 113.5 %all-gather.2.cloned.1.call-start = ((), (), s32[]{:S(2)}) async-start(), calls=%async_computation | async-start | bytes 2654208 | tf_op jit(solution)/shard_map/all_gather | solution.py:45
  9.3 8.2 %collective-permute-start = (f32[144,256]{1,0:T(8,128)S(1)}, f32[144,256]{1,0:T(8,128)S(1)}, u32[]{:S(2)}, u32[]{:S(2)}) collective-permute-start(f32[144,256]{1,0:T(8,128)S(1)} %gather_fusion), channel_id=1, source_target_pairs={{2,0},{4,2},{6,4},{8,6},{10,8},{12,10},{14,12},{16,14},{18,16},{20... | collective-permute-start | bytes 442376 | tf_op jit(solution)/shard_map/ppermute | solution.py:16
  39.9 1.0 copy-start.3
  40.8 7.4 %collective-permute-start.1 = (f32[144,256]{1,0:T(8,128)S(1)}, f32[144,256]{1,0:T(8,128)S(1)}, u32[]{:S(2)}, u32[]{:S(2)}) collective-permute-start(f32[144,256]{1,0:T(8,128)S(1)} %slice.27), channel_id=1, source_target_pairs={{30,0},{0,2},{2,4},{4,6},{6,8},{8,10},{10,12},{12,14},{14,16},{16,... | collective-permute-start | bytes 442376 | tf_op jit(solution)/shard_map/ppermute | solution.py:16
  50.0 4.5 %copy-start.1 = (f32[864,256]{1,0:T(8,128)}, f32[864,256]{1,0:T(8,128)S(1)}, u32[]{:S(2)}) copy-start(f32[864,256]{1,0:T(8,128)S(1)} %scatter_fusion) | copy-start | bytes 2654212
  54.5 2.9 %collective-permute-start.2 = (f32[144,256]{1,0:T(8,128)S(1)}, f32[144,256]{1,0:T(8,128)S(1)}, u32[]{:S(2)}, u32[]{:S(2)}) collective-permute-start(f32[144,256]{1,0:T(8,128)S(1)} %gather_fusion.2), channel_id=1, source_target_pairs={{2,0},{4,2},{6,4},{8,6},{10,8},{12,10},{14,12},{16,14},{18,16},{20... | collective-permute-start | bytes 442376 | tf_op jit(solution)/shard_map/while/body/eval_jaxpr/ppermute | solution.py:16
  79.8 7.5 %collective-permute-start.3 = (f32[144,256]{1,0:T(8,128)S(1)}, f32[144,256]{1,0:T(8,128)S(1)}, u32[]{:S(2)}, u32[]{:S(2)}) collective-permute-start(f32[144,256]{1,0:T(8,128)S(1)} %slice.29), channel_id=1, source_target_pairs={{30,0},{0,2},{2,4},{4,6},{6,8},{8,10},{10,12},{12,14},{14,16},{16,... | collective-permute-start | bytes 442376 | tf_op jit(solution)/shard_map/while/body/eval_jaxpr/ppermute | solution.py:16
  80.8 9.8 %copy-start.2 = (f32[864,256]{1,0:T(8,128)S(1)}, f32[864,256]{1,0:T(8,128)}, u32[]{:S(2)}) copy-start(f32[864,256]{1,0:T(8,128)} %copy-done.1) | copy-start | bytes 2654212
  93.2 127.3 %all-reduce.2.cloned.1.call-start = ((), (), s32[]{:S(2)}) async-start(), calls=%async_computation.1 | async-start | bytes 2097152 | tf_op jit(solution)/shard_map/psum | solution.py:47
Sparse Core Ops, SparseCore 0:
  93.3 26.6 all-gather.1
  126.7 93.6 all-reduce.1
where the time goes:
time: 235 us; the launch traced here: 234 us
  waiting for transfers between devices  138 us (59%)
  other arithmetic  33.1 us (14%)
  local copies, waits for them, and re-layouts  25.3 us (11%)
  matrix products  18 us (8%)
  between operations  14.2 us (6%)
  starting transfers between devices  6.06 us (3%)
    psum x1, waiting for transfers between devices, on_device(): margin = lax.psum(partial_value, 'dom')  93.8 us
    all_gather x1, waiting for transfers between devices, on_device(): full_bands = lax.all_gather(latest, 'band', axis=1, tiled=True)  26.6 us
    scatter-add x2, other arithmetic, local_apply(): jnp.zeros_like(extended).at[flat_map].add(products.reshape(-1, block_width))  17.4 us
    ppermute x4, waiting for transfers between devices, shifted(): return lax.ppermute(block, axis, route)  17.1 us
    gather x2, local copies, waits for them, and re-layouts, local_apply(): extended[flat_map]  9.14 us
    dot_general x2, matrix products, local_apply(): jnp.einsum('cij,cjb->cib', cell_ops, cell_values, precision=lax.Precision...  7.36 us
    dot_general x1, matrix products, on_device(): jnp.einsum('nb,nc->bc', full_bands, full_bands, precision=lax.Precision.H...  6.54 us
    ppermute x4, starting transfers between devices, shifted(): return lax.ppermute(block, axis, route)  5.8 us
  transfers between devices with their start and end apart: 6, of which 6 were waited for; matrix products, arithmetic and copies ran while one was open for 1% of the time, Pallas kernels for 0%

commit v1 on v0

v1 whole, which is shorter than its diff:
```python
import functools
import types

import jax
import jax.numpy as jnp
from jax import lax
from jax.experimental import pallas as pl
from jax.experimental.pallas import tpu as pltpu
from jax.sharding import PartitionSpec as P

DEGREE = 2


cheb_centre = 1.0
cheb_half = 1.6

f32 = jnp.float32
bf16 = jnp.bfloat16
MESH = pl.DeviceIdType.MESH


def round_up(value, step):
    return (value + step - 1) // step * step


def halves(value):
    high = value.astype(bf16)
    low = (value - high.astype(f32)).astype(bf16)
    return high, low


def dot(left, right):
    return jnp.dot(left, right, preferred_element_type=f32)


def dot_tn(left, right):
    return lax.dot_general(left, right, (((0,), (0,)), ((), ())), preferred_element_type=f32)


def dot_nt(left, right):
    return lax.dot_general(left, right, (((1,), (1,)), ((), ())), preferred_element_type=f32)


class Sizes:
    def __init__(self, n_dom, n_band, own, width, cells, nodes, face):
        self.n_dom, self.n_band = n_dom, n_band
        self.own, self.width = own, width
        self.cells, self.nodes, self.face = cells, nodes, face
        self.own_pad = round_up(own, 128)
        self.face_pad = round_up(face, 128)
        self.rows = round_up(nodes, 16)
        self.lanes = round_up(nodes, 128)
        self.half_pad = round_up(own // 2, 128)
        self.chips = n_dom // 2
        self.chunk = width // n_dom
        self.packet = self.chunk + 8
        self.gram = (
            n_band == 2
            and n_dom % 2 == 0
            and n_dom > 2
            and width % (8 * n_dom) == 0
            and width % 128 == 0
            and own % 32 == 0
        )


def start_all(copies):
    for copy in copies:
        copy.start()


def wait_all(copies):
    for copy in copies:
        copy.wait()


def filter_steps(s, ready, wave_ref, ops_ref, map_ref, face_ref, result_ref, w):
    me = lax.axis_index("dom")
    right = lax.rem(me + 1, s.n_dom)
    left = lax.rem(me + s.n_dom - 1, s.n_dom)
    C, R, L, W = s.cells, s.rows, s.lanes, s.width

    def split_store(ref, first, value):
        high, low = halves(value)
        ref[pl.ds(first, value.shape[0]), pl.ds(0, W)] = high
        ref[pl.ds(first, value.shape[0]), pl.ds(W, W)] = low

    def merged(wide):
        return wide[:, :W] + wide[:, W:]

    w.index[...] = jnp.full(w.index.shape, -1.0, f32)
    w.index[pl.ds(0, C), pl.ds(0, s.nodes)] = map_ref[...].astype(f32)
    w.index[pl.ds(C, 1), pl.ds(0, s.face)] = face_ref[...].astype(f32)
    columns = jnp.transpose(w.index[...])

    def one_hot(match):
        return jnp.where(match, 1.0, 0.0).astype(bf16)

    def iota(shape, axis):
        return lax.broadcasted_iota(jnp.int32, shape, axis).astype(f32)

    w.face_rows[...] = one_hot(columns[: s.face, C : C + 1] == iota((s.face, s.own_pad), 1))
    w.vec[pl.ds(s.own, s.own_pad - s.own), :] = jnp.zeros((s.own_pad - s.own, 2 * W), bf16)
    split_store(w.vec, 0, wave_ref[...])

    def face_copy(step):
        return pltpu.make_async_remote_copy(
            src_ref=w.face_send.at[step], dst_ref=w.face_recv.at[step],
            send_sem=w.face_ssem.at[step], recv_sem=w.face_rsem.at[step],
            device_id={"dom": left}, device_id_type=MESH)

    def back_copy(step):
        return pltpu.make_async_remote_copy(
            src_ref=w.back_send.at[step], dst_ref=w.back_recv.at[step],
            send_sem=w.back_ssem.at[step], recv_sem=w.back_rsem.at[step],
            device_id={"dom": right}, device_id_type=MESH)

    w.face_send[0] = merged(dot(w.face_rows[...], w.vec[...]))
    ready()
    face_copy(0).start()

    w.op_pad[...] = jnp.zeros(w.op_pad.shape, f32)
    for c in range(C):
        column = columns[:R, c : c + 1]
        w.take_own[c] = one_hot(column == iota((R, s.own_pad), 1))
        w.take_face[c] = one_hot(column - float(s.own) == iota((R, s.face_pad), 1))
        row = w.index[c : c + 1, :]
        w.put_own[:, pl.ds(c * L, L)] = one_hot(row == iota((s.own, L), 0))
        w.put_face[:, pl.ds(c * L, L)] = one_hot(row - float(s.own) == iota((s.face, L), 0))
        w.op_pad[c, pl.ds(0, s.nodes), pl.ds(0, s.nodes)] = ops_ref[c]
        high, low = halves(w.op_pad[c])
        w.op_high[c] = high
        w.op_low[c] = low
        if L > R:
            w.prod[pl.ds(c * L + R, L - R), :] = jnp.zeros((L - R, 2 * W), bf16)
            w.cell[c, pl.ds(R, L - R), :] = jnp.zeros((L - R, 2 * W), bf16)
    w.put_back[...] = one_hot(w.index[C : C + 1, pl.ds(0, s.face_pad)] == iota((s.own, s.face_pad), 0))
    if s.face_pad > s.face:
        w.far[pl.ds(s.face, s.face_pad - s.face), :] = jnp.zeros((s.face_pad - s.face, 2 * W), bf16)

    for step in range(DEGREE):
        if step > 0:
            split_store(w.vec, 0, w.latest[...])
            w.face_send[step] = merged(dot(w.face_rows[...], w.vec[...]))
            face_copy(step).start()
        for c in range(C):
            w.part[c] = dot(w.take_own[c], w.vec[...])
        face_copy(step).wait()
        split_store(w.far, 0, w.face_recv[step])
        for c in range(C):
            cell = w.part[c] + dot(w.take_face[c], w.far[...])
            w.cell[c, pl.ds(0, R), :] = cell.astype(bf16)
            wide = dot(w.op_high[c], w.cell[c])
            value = wide[:, :W] + wide[:, W:] + dot(w.op_low[c], w.cell[c, :, pl.ds(0, W)])
            split_store(w.prod, c * L, value)
        w.back_send[step] = merged(dot(w.put_face[...], w.prod[...]))
        back_copy(step).start()
        applied = merged(dot(w.put_own[...], w.prod[...]))
        back_copy(step).wait()
        split_store(w.far, 0, w.back_recv[step])
        applied = applied + merged(dot(w.put_back[...], w.far[...]))
        current = wave_ref[...] if step == 0 else w.latest[...]
        if step == 0:
            following = (applied - cheb_centre * current) / cheb_half
        else:
            earlier = wave_ref[...] if step == 1 else w.older[...]
            following = 2.0 * (applied - cheb_centre * current) / cheb_half - earlier
        if step == DEGREE - 1:
            result_ref[...] = following
        else:
            if step > 0 and step < DEGREE - 1:
                w.older[...] = current
            w.latest[...] = following


def gram_steps(s, band_ref, out_ref, w):
    me = lax.axis_index("dom")
    band = lax.axis_index("band")
    other = 1 - band
    chip, core = me // 2, lax.rem(me, 2)
    partner = chip * 2 + (1 - core)
    W, half, n, chunk = s.width, s.own // 2, s.chips, s.chunk

    def band_copy(turn, first):
        rows = pl.ds(pl.multiple_of(first * half, 8), half)
        return pltpu.make_async_remote_copy(
            src_ref=band_ref.at[rows, :], dst_ref=w.far_band.at[rows, :],
            send_sem=w.band_ssem.at[turn], recv_sem=w.band_rsem.at[turn],
            device_id={"band": other}, device_id_type=MESH)

    def core_copy(m):
        return pltpu.make_async_remote_copy(
            src_ref=w.sums.at[m, 1 - core], dst_ref=w.core_recv.at[m],
            send_sem=w.core_ssem.at[m], recv_sem=w.core_rsem.at[m],
            device_id={"dom": partner}, device_id_type=MESH)

    def scatter_copies(m):
        copies = []
        for j in range(1, n):
            target = lax.rem(chip + j, n)
            copies.append(pltpu.make_async_remote_copy(
                src_ref=w.pair.at[m, target], dst_ref=w.scat_recv.at[m, j - 1],
                send_sem=w.scat_ssem.at[m, j - 1], recv_sem=w.scat_rsem.at[m, j - 1],
                device_id={"dom": target * 2 + core}, device_id_type=MESH))
        return copies

    def gather_copies(m):
        copies = []
        for j in range(1, n):
            target = lax.rem(chip + j, n)
            copies.append(pltpu.make_async_remote_copy(
                src_ref=w.full.at[m, core, chip], dst_ref=w.full.at[m, core, chip],
                send_sem=w.gath_ssem.at[m, j - 1], recv_sem=w.gath_rsem.at[m, j - 1],
                device_id={"dom": target * 2 + core}, device_id_type=MESH))
        return copies

    def swap_copy(m):
        return pltpu.make_async_remote_copy(
            src_ref=w.full.at[m, core], dst_ref=w.full.at[m, core],
            send_sem=w.swap_ssem.at[m], recv_sem=w.swap_rsem.at[m],
            device_id={"dom": partner}, device_id_type=MESH)

    def cross_copy():
        return pltpu.make_async_remote_copy(
            src_ref=w.cross_send, dst_ref=w.cross_recv,
            send_sem=w.cross_ssem, recv_sem=w.cross_rsem,
            device_id={"band": other}, device_id_type=MESH)

    def put_sums(m, value):
        w.sums[m] = value.reshape(2, W // 2, W)

    def pair_up(m):
        core_copy(m).wait()
        total = w.sums[m, core] + w.core_recv[m]
        w.pair[m] = total.reshape(n, chunk, W)

    def own_total(m):
        wait_all(scatter_copies(m))
        total = w.pair[m, chip]
        for j in range(n - 1):
            total = total + w.scat_recv[m, j]
        return total

    band_copy(0, other).start()
    high, low = halves(band_ref[...])
    def fill(ref, value):
        count, size = value.shape[0], ref.shape[0]
        ref[pl.ds(0, count), :] = value
        if size > count:
            ref[pl.ds(count, size - count), :] = jnp.zeros((size - count, W), bf16)

    fill(w.near_high, high)
    fill(w.near_low, low)
    turned_high, turned_low = halves(jnp.transpose(w.bands[...]))
    put_sums(0, dot(turned_high, w.near_high[...])
             + dot(turned_high, w.near_low[...])
             + dot(turned_low, w.near_high[...]))
    core_copy(0).start()
    pair_up(0)
    start_all(scatter_copies(0))
    same = own_total(0)
    w.full[0, core, chip, pl.ds(0, chunk), :] = same
    squares = (same * same).reshape(chunk // 8, 8, W).sum(0)
    w.full[0, core, chip, pl.ds(chunk, 8), :] = squares
    start_all(gather_copies(0))

    band_copy(0, other).wait_send()
    band_copy(0, band).wait_recv()
    band_copy(1, band).start()
    rows = pl.ds(pl.multiple_of(band * half, 16), half)
    far_high, far_low = halves(w.far_band[rows, :])
    near_high, near_low = w.near_high[rows, :], w.near_low[rows, :]
    first = band == 0

    def pick(a, b):
        return jnp.where(first, a, b)

    fill(w.left_high, pick(far_high, near_high))
    fill(w.left_low, pick(far_low, near_low))
    fill(w.right_high, pick(near_high, far_high))
    fill(w.right_low, pick(near_low, far_low))
    put_sums(1, dot_tn(w.left_high[...], w.right_high[...])
             + dot_tn(w.left_high[...], w.right_low[...])
             + dot_tn(w.left_low[...], w.right_high[...]))
    core_copy(1).start()
    pair_up(1)
    start_all(scatter_copies(1))

    wait_all(gather_copies(0))
    swap_copy(0).start()
    cross = own_total(1)
    w.cross_send[pl.ds(0, chunk), :] = cross
    w.cross_send[pl.ds(chunk, 8), :] = squares
    cross_copy().start()
    cross_copy().wait()
    cross = pick(cross, w.cross_recv[pl.ds(0, chunk), :]) + pick(w.cross_recv[pl.ds(0, chunk), :], cross)
    w.full[1, core, chip, pl.ds(0, chunk), :] = cross
    w.full[1, core, chip, pl.ds(chunk, 8), :] = (
        2.0 * (cross * cross).reshape(chunk // 8, 8, W).sum(0) + w.cross_recv[pl.ds(chunk, 8), :])
    start_all(gather_copies(1))
    swap_copy(0).wait()
    near_block = w.full[0, :, :, pl.ds(0, chunk), :].reshape(W, W)
    block_high, block_low = halves(near_block)
    w.block_high[0] = block_high
    w.block_low[0] = block_low
    near_high, near_low = w.near_high[pl.ds(0, s.own), :], w.near_low[pl.ds(0, s.own), :]
    near_wide = dot(near_high, w.block_high[0]) + dot(near_high, w.block_low[0])
    w.near_prod[...] = near_wide + dot(near_low, w.block_high[0])
    band_copy(1, band).wait_send()
    band_copy(1, other).wait_recv()
    high, low = halves(w.far_band[...])
    w.far_high[...] = high
    w.far_low[...] = low
    wait_all(gather_copies(1))
    swap_copy(1).start()
    swap_copy(1).wait()
    total = jnp.sum(w.full[:, :, :, pl.ds(chunk, 8), :])
    norm = jnp.sqrt(jnp.full((1, W), total, f32) + 1e-06)
    far_block = w.full[1, :, :, pl.ds(0, chunk), :].reshape(W, W)
    far_block = pick(far_block, jnp.transpose(far_block))
    block_high, block_low = halves(far_block)
    w.block_high[1] = block_high
    w.block_low[1] = block_low
    wide = dot(w.far_high[...], w.block_high[1]) + dot(w.far_high[...], w.block_low[1])
    wide = wide + dot(w.far_low[...], w.block_high[1]) + w.near_prod[...]
    out_ref[...] = 1.5 * band_ref[...] - wide * (0.5 / norm)


def kernel(s, names, wave_ref, ops_ref, map_ref, face_ref, out_ref, *scratch):
    w = types.SimpleNamespace(**dict(zip(names, scratch)))
    me = lax.axis_index("dom")
    barrier = pltpu.get_barrier_semaphore()
    greeted = [{"dom": lax.rem(me + 1, s.n_dom)}, {"dom": lax.rem(me + s.n_dom - 1, s.n_dom)}]
    if s.gram:
        chip, core = me // 2, lax.rem(me, 2)
        greeted.append({"dom": chip * 2 + (1 - core)})
        greeted.append({"band": 1 - lax.axis_index("band")})
        for j in range(1, s.chips):
            greeted.append({"dom": lax.rem(chip + j, s.chips) * 2 + core})
    for device in greeted:
        pl.semaphore_signal(barrier, inc=1, device_id=device, device_id_type=MESH)

    def ready():
        pl.semaphore_wait(barrier, len(greeted))

    if s.gram:
        if s.own_pad > s.own:
            w.bands[pl.ds(s.own, s.own_pad - s.own), :] = jnp.zeros((s.own_pad - s.own, s.width), f32)
        owned = w.bands.at[pl.ds(0, s.own), :]
        filter_steps(s, ready, wave_ref, ops_ref, map_ref, face_ref, owned, w)
        gram_steps(s, owned, out_ref, w)
    else:
        filter_steps(s, ready, wave_ref, ops_ref, map_ref, face_ref, out_ref, w)


def scratch_of(s):
    C, R, L, W, n, chunk = s.cells, s.rows, s.lanes, s.width, s.chips, s.chunk
    V, dma = pltpu.VMEM, pltpu.SemaphoreType.DMA
    scratch = dict(
        index=V((128, max(L, s.face_pad)), f32),
        face_rows=V((s.face, s.own_pad), bf16),
        vec=V((s.own_pad, 2 * W), bf16),
        take_own=V((C, R, s.own_pad), bf16),
        take_face=V((C, R, s.face_pad), bf16),
        put_own=V((s.own, C * L), bf16),
        put_face=V((s.face, C * L), bf16),
        put_back=V((s.own, s.face_pad), bf16),
        op_pad=V((C, R, L), f32),
        op_high=V((C, R, L), bf16),
        op_low=V((C, R, L), bf16),
        part=V((C, R, 2 * W), f32),
        cell=V((C, L, 2 * W), bf16),
        prod=V((C * L, 2 * W), bf16),
        far=V((s.face_pad, 2 * W), bf16),
        latest=V((s.own, W), f32),
        older=V((s.own, W) if DEGREE > 2 else (8, 128), f32),
        face_send=V((DEGREE, s.face, W), f32),
        face_recv=V((DEGREE, s.face, W), f32),
        back_send=V((DEGREE, s.face, W), f32),
        back_recv=V((DEGREE, s.face, W), f32),
        face_ssem=dma((DEGREE,)),
        face_rsem=dma((DEGREE,)),
        back_ssem=dma((DEGREE,)),
        back_rsem=dma((DEGREE,)),
    )
    if s.gram:
        scratch |= dict(
            bands=V((s.own_pad, W), f32),
            far_band=V((s.own, W), f32),
            near_high=V((s.own_pad, W), bf16),
            near_low=V((s.own_pad, W), bf16),
            left_high=V((s.half_pad, W), bf16),
            left_low=V((s.half_pad, W), bf16),
            right_high=V((s.half_pad, W), bf16),
            right_low=V((s.half_pad, W), bf16),
            far_high=V((s.own, W), bf16),
            far_low=V((s.own, W), bf16),
            near_prod=V((s.own, W), f32),
            block_high=V((2, W, W), bf16),
            block_low=V((2, W, W), bf16),
            sums=V((2, 2, W // 2, W), f32),
            core_recv=V((2, W // 2, W), f32),
            pair=V((2, n, chunk, W), f32),
            scat_recv=V((2, n - 1, chunk, W), f32),
            full=V((2, 2, n, s.packet, W), f32),
            cross_send=V((s.packet, W), f32),
            cross_recv=V((s.packet, W), f32),
            cross_ssem=dma,
            cross_rsem=dma,
            band_ssem=dma((2,)),
            band_rsem=dma((2,)),
            core_ssem=dma((2,)),
            core_rsem=dma((2,)),
            swap_ssem=dma((2,)),
            swap_rsem=dma((2,)),
            scat_ssem=dma((2, n - 1)),
            scat_rsem=dma((2, n - 1)),
            gath_ssem=dma((2, n - 1)),
            gath_rsem=dma((2, n - 1)),
        )
    return scratch


def on_device(wavefun, cell_ops, cell_map, face_list):
    s = Sizes(lax.axis_size("dom"), lax.axis_size("band"), wavefun.shape[0], wavefun.shape[1],
              cell_map.shape[0], cell_map.shape[1], face_list.shape[0])
    scratch = scratch_of(s)
    latest = pl.pallas_call(
        functools.partial(kernel, s, list(scratch)),
        out_shape=jax.ShapeDtypeStruct(wavefun.shape, f32),
        in_specs=[pl.BlockSpec(memory_space=pltpu.VMEM)] * 4,
        out_specs=pl.BlockSpec(memory_space=pltpu.VMEM),
        scratch_shapes=list(scratch.values()),
        compiler_params=pltpu.CompilerParams(
            collective_id=0, has_side_effects=True, vmem_limit_bytes=60 * 1024 * 1024),
        name="filtered_bands",
    )(wavefun, cell_ops, cell_map, face_list.reshape(1, -1))
    if s.gram:
        return latest
    full_bands = lax.all_gather(latest, "band", axis=1, tiled=True)
    partial_value = jnp.einsum("nb,nc->bc", full_bands, full_bands, precision=lax.Precision.HIGHEST)
    margin = lax.psum(partial_value, "dom")
    norm_value = jnp.sqrt(jnp.sum(margin * margin) + 1e-06)
    full_width = margin.shape[0]
    offset = lax.axis_index("band") * s.width
    scaled_cols = lax.dynamic_slice_in_dim(margin, offset, s.width, 1) / norm_value
    identity_cols = lax.dynamic_slice_in_dim(
        jnp.eye(full_width, dtype=jnp.float32), offset, s.width, 1
    )
    mixing = (3.0 * identity_cols - scaled_cols) / 2.0
    return jnp.dot(full_bands, mixing, precision=lax.Precision.HIGHEST)


def solution(mesh):
    return jax.shard_map(
        on_device,
        mesh=mesh,
        in_specs=(P("dom", "band"), P("dom", None, None), P("dom", None), P("dom")),
        out_specs=P("dom", "band"),
        check_vma=False,
    )
```

time: 235 us -> 68.8 us (0.29)
  waiting for transfers between devices: 138 us -> 0 us
  Pallas kernels: 0 us -> 63.3 us
  other arithmetic: 33.1 us -> 0 us
  local copies, waits for them, and re-layouts: 25.3 us -> 5.22 us
  matrix products: 18 us -> 0 us
  between operations: 14.2 us -> 0.01 us
  starting transfers between devices: 6.06 us -> 0 us
    psum x1 -> x0, waiting for transfers between devices: 93.8 us -> none  [on_device(): margin = lax.psum(partial_value, 'dom')]
    pallas_call x0 -> x1, Pallas kernels: none -> 63.3 us  [on_device(): pl.pallas_call(functools.partial(kernel, s, list(scratch)), out_shape=jax...]
    all_gather x1 -> x0, waiting for transfers between devices: 26.6 us -> none  [on_device(): full_bands = lax.all_gather(latest, 'band', axis=1, tiled=True)]
    scatter-add x4 -> x0, other arithmetic: 22.4 us -> none  [the longest x2 17.4 us: local_apply(): jnp.zeros_like(extended).at[flat_map].add(products.reshape(-1, block_width))]
    dot_general x4 -> x0, matrix products: 18 us -> none  [the longest x2 7.36 us: local_apply(): jnp.einsum('cij,cjb->cib', cell_ops, cell_values, precision=lax.Precision...]
    ppermute x4 -> x0, waiting for transfers between devices: 17.1 us -> none  [shifted(): return lax.ppermute(block, axis, route)]
    gather x4 -> x0, local copies, waits for them, and re-layouts: 13 us -> none  [the longest x2 9.14 us: local_apply(): extended[flat_map]]
    reshape x5 -> x0, local copies, waits for them, and re-layouts: 9.02 us -> none  [the longest x2 5.23 us: local_apply(): products.reshape(-1, block_width)]
  transfers between devices with their start and end apart: 6 -> 0, of which waited for: 6 -> 0; matrix products, arithmetic and copies ran while one was open for 1% -> 0% of each run, Pallas kernels for 0% -> 0%
where the time goes in v1:
time: 68.8 us; the launch traced here: 68.6 us
  Pallas kernels  63.3 us (92%)
  local copies, waits for them, and re-layouts  5.22 us (8%)
    pallas_call x1, Pallas kernels, on_device(): pl.pallas_call(functools.partial(kernel, s, list(scratch)), out_shape=jax...  63.3 us
    unnamed x2, local copies, waits for them, and re-layouts  5.22 us

profile of v1, /device:TPU:0, one launch (start us, length us, event | category | flops | bytes accessed | tf_op | source)
XLA Modules:
  0.0 68.6 jit_solution(7846121900683281334)
XLA Ops:
  0.0 3.1 %copy.5.ops_ref = f32[4,343,343]{2,1,0:T(8,128)} copy(f32[4,343,343]{2,0,1:T(4,128)} %param.5) | data formatting | bytes 3764768 | tf_op args[1]
  3.1 63.3 %filtered_bands.1 = f32[864,256]{1,0:T(8,128)} custom-call(f32[864,256]{1,0:T(8,128)} %wave_ref.1, f32[4,343,343]{2,1,0:T(8,128)} %copy.5.ops_ref, s32[4,343]{1,0:T(4,128)} %map_ref.1, s32[1,144]{1,0:T(1,128)} %bitcast.1), custom_call_target="tpu_custom_call" | custom-call | tf_op jit(solution)/shard_map/filtered_bands/pallas_call | solution.py:428
  66.4 2.1 %copy.7 = f32[864,256]{1,0:T(8,128)} copy(f32[864,256]{1,0:T(8,128)} %filtered_bands.1) | data formatting | bytes 1769472

commit v2 on v1

--- a/solution.py
+++ b/solution.py
@@ -88,6 +88,12 @@
     def merged(wide):
         return wide[:, :W] + wide[:, W:]
 
+    def ops_copy(c):
+        return pltpu.make_async_copy(ops_ref.at[c], w.ops.at[c], w.ops_sem.at[c])
+
+    for c in range(C):
+        ops_copy(c).start()
+
     w.index[...] = jnp.full(w.index.shape, -1.0, f32)
     w.index[pl.ds(0, C), pl.ds(0, s.nodes)] = map_ref[...].astype(f32)
     w.index[pl.ds(C, 1), pl.ds(0, s.face)] = face_ref[...].astype(f32)
@@ -127,7 +133,8 @@
         row = w.index[c : c + 1, :]
         w.put_own[:, pl.ds(c * L, L)] = one_hot(row == iota((s.own, L), 0))
         w.put_face[:, pl.ds(c * L, L)] = one_hot(row - float(s.own) == iota((s.face, L), 0))
-        w.op_pad[c, pl.ds(0, s.nodes), pl.ds(0, s.nodes)] = ops_ref[c]
+        ops_copy(c).wait()
+        w.op_pad[c, pl.ds(0, s.nodes), pl.ds(0, s.nodes)] = w.ops[c]
         high, low = halves(w.op_pad[c])
         w.op_high[c] = high
         w.op_low[c] = low
@@ -365,6 +372,8 @@
         put_own=V((s.own, C * L), bf16),
         put_face=V((s.face, C * L), bf16),
         put_back=V((s.own, s.face_pad), bf16),
+        ops=V((C, s.nodes, s.nodes), f32),
+        ops_sem=dma((C,)),
         op_pad=V((C, R, L), f32),
         op_high=V((C, R, L), bf16),
         op_low=V((C, R, L), bf16),
@@ -428,7 +437,7 @@
     latest = pl.pallas_call(
         functools.partial(kernel, s, list(scratch)),
         out_shape=jax.ShapeDtypeStruct(wavefun.shape, f32),
-        in_specs=[pl.BlockSpec(memory_space=pltpu.VMEM)] * 4,
+        in_specs=[pl.BlockSpec(memory_space=space) for space in (pltpu.VMEM, pl.ANY, pltpu.VMEM, pltpu.VMEM)],
         out_specs=pl.BlockSpec(memory_space=pltpu.VMEM),
         scratch_shapes=list(scratch.values()),
         compiler_params=pltpu.CompilerParams(

time: 68.8 us -> 68.2 us (level)
  no operation moved by 1% of the time
where the time goes in v2:
time: 68.2 us; the launch traced here: 68 us
  Pallas kernels  62.7 us (92%)
  local copies, waits for them, and re-layouts  5.22 us (8%)
    pallas_call x1, Pallas kernels, on_device(): pl.pallas_call(functools.partial(kernel, s, list(scratch)), out_shape=jax...  62.7 us
    unnamed x2, local copies, waits for them, and re-layouts  5.22 us

profile of v2, /device:TPU:0, one launch (start us, length us, event | category | flops | bytes accessed | tf_op | source)
XLA Modules:
  0.0 68.0 jit_solution(8099254184044049447)
XLA Ops:
  0.0 3.1 %copy.5.ops_ref = f32[4,343,343]{2,1,0:T(8,128)} copy(f32[4,343,343]{2,0,1:T(4,128)} %param.5) | data formatting | bytes 3764768 | tf_op args[1]
  3.1 62.7 %filtered_bands.1 = f32[864,256]{1,0:T(8,128)} custom-call(f32[864,256]{1,0:T(8,128)} %wave_ref.1, f32[4,343,343]{2,1,0:T(8,128)} %copy.5.ops_ref, s32[4,343]{1,0:T(4,128)} %map_ref.1, s32[1,144]{1,0:T(1,128)} %bitcast.1), custom_call_target="tpu_custom_call" | custom-call | tf_op jit(solution)/shard_map/filtered_bands/pallas_call | solution.py:437
  65.8 2.1 %copy.7 = f32[864,256]{1,0:T(8,128)} copy(f32[864,256]{1,0:T(8,128)} %filtered_bands.1) | data formatting | bytes 1769472

commit v3 on v2

--- a/solution.py
+++ b/solution.py
@@ -50,6 +50,8 @@
         self.face_pad = round_up(face, 128)
         self.rows = round_up(nodes, 16)
         self.lanes = round_up(nodes, 128)
+        self.blocks = 2 if width % 256 == 0 else 1
+        self.block = width // self.blocks
         self.half_pad = round_up(own // 2, 128)
         self.chips = n_dom // 2
         self.chunk = width // n_dom
@@ -74,11 +76,11 @@
         copy.wait()
 
 
-def filter_steps(s, ready, wave_ref, ops_ref, map_ref, face_ref, result_ref, w):
+def filter_steps(s, ready, done, wave_ref, ops_ref, map_ref, face_ref, result_ref, w):
     me = lax.axis_index("dom")
     right = lax.rem(me + 1, s.n_dom)
     left = lax.rem(me + s.n_dom - 1, s.n_dom)
-    C, R, L, W = s.cells, s.rows, s.lanes, s.width
+    C, R, L, W = s.cells, s.rows, s.lanes, s.block
 
     def split_store(ref, first, value):
         high, low = halves(value)
@@ -106,24 +108,31 @@
         return lax.broadcasted_iota(jnp.int32, shape, axis).astype(f32)
 
     w.face_rows[...] = one_hot(columns[: s.face, C : C + 1] == iota((s.face, s.own_pad), 1))
-    w.vec[pl.ds(s.own, s.own_pad - s.own), :] = jnp.zeros((s.own_pad - s.own, 2 * W), bf16)
-    split_store(w.vec, 0, wave_ref[...])
-
-    def face_copy(step):
+    for q in range(s.blocks):
+        if s.own_pad > s.own:
+            w.vec[q, pl.ds(s.own, s.own_pad - s.own), :] = jnp.zeros((s.own_pad - s.own, 2 * W), bf16)
+        split_store(w.vec.at[q], 0, wave_ref[:, pl.ds(q * W, W)])
+
+    def face_copy(step, q):
         return pltpu.make_async_remote_copy(
-            src_ref=w.face_send.at[step], dst_ref=w.face_recv.at[step],
-            send_sem=w.face_ssem.at[step], recv_sem=w.face_rsem.at[step],
+            src_ref=w.face_send.at[step, q], dst_ref=w.face_recv.at[step, q],
+            send_sem=w.face_ssem.at[step, q], recv_sem=w.face_rsem.at[step, q],
             device_id={"dom": left}, device_id_type=MESH)
 
-    def back_copy(step):
+    def back_copy(step, q):
         return pltpu.make_async_remote_copy(
-            src_ref=w.back_send.at[step], dst_ref=w.back_recv.at[step],
-            send_sem=w.back_ssem.at[step], recv_sem=w.back_rsem.at[step],
+            src_ref=w.back_send.at[step, q], dst_ref=w.back_recv.at[step, q],
+            send_sem=w.back_ssem.at[step, q], recv_sem=w.back_rsem.at[step, q],
             device_id={"dom": right}, device_id_type=MESH)
 
-    w.face_send[0] = merged(dot(w.face_rows[...], w.vec[...]))
-    ready()
-    face_copy(0).start()
+    def begin(step, q):
+        w.face_send[step, q] = merged(dot(w.face_rows[...], w.vec[q]))
+        if step == 0 and q == 0:
+            ready()
+        face_copy(step, q).start()
+
+    for q in range(s.blocks):
+        begin(0, q)
 
     w.op_pad[...] = jnp.zeros(w.op_pad.shape, f32)
     for c in range(C):
@@ -143,41 +152,71 @@
             w.cell[c, pl.ds(R, L - R), :] = jnp.zeros((L - R, 2 * W), bf16)
     w.put_back[...] = one_hot(w.index[C : C + 1, pl.ds(0, s.face_pad)] == iota((s.own, s.face_pad), 0))
     if s.face_pad > s.face:
-        w.far[pl.ds(s.face, s.face_pad - s.face), :] = jnp.zeros((s.face_pad - s.face, 2 * W), bf16)
-
-    for step in range(DEGREE):
-        if step > 0:
-            split_store(w.vec, 0, w.latest[...])
-            w.face_send[step] = merged(dot(w.face_rows[...], w.vec[...]))
-            face_copy(step).start()
+        for q in range(s.blocks):
+            w.far[q, pl.ds(s.face, s.face_pad - s.face), :] = jnp.zeros((s.face_pad - s.face, 2 * W), bf16)
+
+    def gather(step, q):
         for c in range(C):
-            w.part[c] = dot(w.take_own[c], w.vec[...])
-        face_copy(step).wait()
-        split_store(w.far, 0, w.face_recv[step])
+            w.part[q, c] = dot(w.take_own[c], w.vec[q])
+
+    def middle(step, q):
+        face_copy(step, q).wait()
+        split_store(w.far.at[q], 0, w.face_recv[step, q])
         for c in range(C):
-            cell = w.part[c] + dot(w.take_face[c], w.far[...])
+            cell = w.part[q, c] + dot(w.take_face[c], w.far[q])
             w.cell[c, pl.ds(0, R), :] = cell.astype(bf16)
             wide = dot(w.op_high[c], w.cell[c])
             value = wide[:, :W] + wide[:, W:] + dot(w.op_low[c], w.cell[c, :, pl.ds(0, W)])
             split_store(w.prod, c * L, value)
-        w.back_send[step] = merged(dot(w.put_face[...], w.prod[...]))
-        back_copy(step).start()
-        applied = merged(dot(w.put_own[...], w.prod[...]))
-        back_copy(step).wait()
-        split_store(w.far, 0, w.back_recv[step])
-        applied = applied + merged(dot(w.put_back[...], w.far[...]))
-        current = wave_ref[...] if step == 0 else w.latest[...]
+        w.back_send[step, q] = merged(dot(w.put_face[...], w.prod[...]))
+        back_copy(step, q).start()
+        w.applied[q] = merged(dot(w.put_own[...], w.prod[...]))
+
+    def finish(step, q):
+        back_copy(step, q).wait()
+        split_store(w.far.at[q], 0, w.back_recv[step, q])
+        applied = w.applied[q] + merged(dot(w.put_back[...], w.far[q]))
+        columns = pl.ds(q * W, W)
         if step == 0:
+            current = wave_ref[:, columns]
             following = (applied - cheb_centre * current) / cheb_half
         else:
-            earlier = wave_ref[...] if step == 1 else w.older[...]
+            current = w.latest[:, columns]
+            earlier = wave_ref[:, columns] if step == 1 else w.older[:, columns]
             following = 2.0 * (applied - cheb_centre * current) / cheb_half - earlier
         if step == DEGREE - 1:
-            result_ref[...] = following
+            result_ref[:, columns] = following
+            done(q)
         else:
-            if step > 0 and step < DEGREE - 1:
-                w.older[...] = current
-            w.latest[...] = following
+            if step > 0:
+                w.older[:, columns] = current
+            w.latest[:, columns] = following
+            split_store(w.vec.at[q], 0, following)
+            begin(step + 1, q)
+
+    gather(0, 0)
+    for step in range(DEGREE):
+        last = step == DEGREE - 1
+        middle(step, 0)
+        if s.blocks > 1:
+            gather(step, 1)
+        finish(step, 0)
+        if s.blocks > 1:
+            middle(step, 1)
+        if not last:
+            gather(step + 1, 0)
+        if s.blocks > 1:
+            finish(step, 1)
+
+
+def band_copy(s, band_ref, w, turn, first, q):
+    half = s.own // 2
+    rows = pl.ds(pl.multiple_of(first * half, 8), half)
+    columns = pl.ds(q * s.block, s.block)
+    return pltpu.make_async_remote_copy(
+        src_ref=band_ref.at[rows, columns], dst_ref=w.far_band.at[rows, columns],
+        send_sem=w.band_ssem.at[turn, q], recv_sem=w.band_rsem.at[turn, q],
+        device_id={"band": 1 - lax.axis_index("band")}, device_id_type=MESH)
 
 
 def gram_steps(s, band_ref, out_ref, w):
@@ -187,13 +226,6 @@
     chip, core = me // 2, lax.rem(me, 2)
     partner = chip * 2 + (1 - core)
     W, half, n, chunk = s.width, s.own // 2, s.chips, s.chunk
-
-    def band_copy(turn, first):
-        rows = pl.ds(pl.multiple_of(first * half, 8), half)
-        return pltpu.make_async_remote_copy(
-            src_ref=band_ref.at[rows, :], dst_ref=w.far_band.at[rows, :],
-            send_sem=w.band_ssem.at[turn], recv_sem=w.band_rsem.at[turn],
-            device_id={"band": other}, device_id_type=MESH)
 
     def core_copy(m):
         return pltpu.make_async_remote_copy(
@@ -248,7 +280,6 @@
             total = total + w.scat_recv[m, j]
         return total
 
-    band_copy(0, other).start()
     high, low = halves(band_ref[...])
     def fill(ref, value):
         count, size = value.shape[0], ref.shape[0]
@@ -271,9 +302,11 @@
     w.full[0, core, chip, pl.ds(chunk, 8), :] = squares
     start_all(gather_copies(0))
 
-    band_copy(0, other).wait_send()
-    band_copy(0, band).wait_recv()
-    band_copy(1, band).start()
+    for q in range(s.blocks):
+        band_copy(s, band_ref, w, 0, other, q).wait_send()
+        band_copy(s, band_ref, w, 0, band, q).wait_recv()
+    for q in range(s.blocks):
+        band_copy(s, band_ref, w, 1, band, q).start()
     rows = pl.ds(pl.multiple_of(band * half, 16), half)
     far_high, far_low = halves(w.far_band[rows, :])
     near_high, near_low = w.near_high[rows, :], w.near_low[rows, :]
@@ -313,8 +346,9 @@
     near_high, near_low = w.near_high[pl.ds(0, s.own), :], w.near_low[pl.ds(0, s.own), :]
     near_wide = dot(near_high, w.block_high[0]) + dot(near_high, w.block_low[0])
     w.near_prod[...] = near_wide + dot(near_low, w.block_high[0])
-    band_copy(1, band).wait_send()
-    band_copy(1, other).wait_recv()
+    for q in range(s.blocks):
+        band_copy(s, band_ref, w, 1, band, q).wait_send()
+        band_copy(s, band_ref, w, 1, other, q).wait_recv()
     high, low = halves(w.far_band[...])
     w.far_high[...] = high
     w.far_low[...] = low
@@ -354,10 +388,14 @@
         if s.own_pad > s.own:
             w.bands[pl.ds(s.own, s.own_pad - s.own), :] = jnp.zeros((s.own_pad - s.own, s.width), f32)
         owned = w.bands.at[pl.ds(0, s.own), :]
-        filter_steps(s, ready, wave_ref, ops_ref, map_ref, face_ref, owned, w)
+
+        def send(q):
+            band_copy(s, owned, w, 0, 1 - lax.axis_index("band"), q).start()
+
+        filter_steps(s, ready, send, wave_ref, ops_ref, map_ref, face_ref, owned, w)
         gram_steps(s, owned, out_ref, w)
     else:
-        filter_steps(s, ready, wave_ref, ops_ref, map_ref, face_ref, out_ref, w)
+        filter_steps(s, ready, lambda q: None, wave_ref, ops_ref, map_ref, face_ref, out_ref, w)
 
 
 def scratch_of(s):
@@ -366,7 +404,7 @@
     scratch = dict(
         index=V((128, max(L, s.face_pad)), f32),
         face_rows=V((s.face, s.own_pad), bf16),
-        vec=V((s.own_pad, 2 * W), bf16),
+        vec=V((s.blocks, s.own_pad, 2 * s.block), bf16),
         take_own=V((C, R, s.own_pad), bf16),
         take_face=V((C, R, s.face_pad), bf16),
         put_own=V((s.own, C * L), bf16),
@@ -377,20 +415,21 @@
         op_pad=V((C, R, L), f32),
         op_high=V((C, R, L), bf16),
         op_low=V((C, R, L), bf16),
-        part=V((C, R, 2 * W), f32),
-        cell=V((C, L, 2 * W), bf16),
-        prod=V((C * L, 2 * W), bf16),
-        far=V((s.face_pad, 2 * W), bf16),
+        part=V((s.blocks, C, R, 2 * s.block), f32),
+        applied=V((s.blocks, s.own, s.block), f32),
+        cell=V((C, L, 2 * s.block), bf16),
+        prod=V((C * L, 2 * s.block), bf16),
+        far=V((s.blocks, s.face_pad, 2 * s.block), bf16),
         latest=V((s.own, W), f32),
         older=V((s.own, W) if DEGREE > 2 else (8, 128), f32),
-        face_send=V((DEGREE, s.face, W), f32),
-        face_recv=V((DEGREE, s.face, W), f32),
-        back_send=V((DEGREE, s.face, W), f32),
-        back_recv=V((DEGREE, s.face, W), f32),
-        face_ssem=dma((DEGREE,)),
-        face_rsem=dma((DEGREE,)),
-        back_ssem=dma((DEGREE,)),
-        back_rsem=dma((DEGREE,)),
+        face_send=V((DEGREE, s.blocks, s.face, s.block), f32),
+        face_recv=V((DEGREE, s.blocks, s.face, s.block), f32),
+        back_send=V((DEGREE, s.blocks, s.face, s.block), f32),
+        back_recv=V((DEGREE, s.blocks, s.face, s.block), f32),
+        face_ssem=dma((DEGREE, s.blocks)),
+        face_rsem=dma((DEGREE, s.blocks)),
+        back_ssem=dma((DEGREE, s.blocks)),
+        back_rsem=dma((DEGREE, s.blocks)),
     )
     if s.gram:
         scratch |= dict(
@@ -416,8 +455,8 @@
             cross_recv=V((s.packet, W), f32),
             cross_ssem=dma,
             cross_rsem=dma,
-            band_ssem=dma((2,)),
-            band_rsem=dma((2,)),
+            band_ssem=dma((2, s.blocks)),
+            band_rsem=dma((2, s.blocks)),
             core_ssem=dma((2,)),
             core_rsem=dma((2,)),
             swap_ssem=dma((2,)),

time: 68.2 us -> 66.9 us (0.981)
  Pallas kernels: 62.7 us -> 61.5 us
    pallas_call x1, Pallas kernels: 62.7 us -> 61.5 us  [on_device(): pl.pallas_call(functools.partial(kernel, s, list(scratch)), out_shape=jax...]
where the time goes in v3:
time: 66.9 us; the launch traced here: 66.7 us
  Pallas kernels  61.5 us (92%)
  local copies, waits for them, and re-layouts  5.22 us (8%)
    pallas_call x1, Pallas kernels, on_device(): pl.pallas_call(functools.partial(kernel, s, list(scratch)), out_shape=jax...  61.5 us
    unnamed x2, local copies, waits for them, and re-layouts  5.22 us

profile of v3, /device:TPU:0, one launch (start us, length us, event | category | flops | bytes accessed | tf_op | source)
XLA Modules:
  0.0 66.7 jit_solution(10547787868821865604)
XLA Ops:
  0.0 3.1 %copy.5.ops_ref = f32[4,343,343]{2,1,0:T(8,128)} copy(f32[4,343,343]{2,0,1:T(4,128)} %param.5) | data formatting | bytes 3764768 | tf_op args[1]
  3.1 61.5 %filtered_bands.1 = f32[864,256]{1,0:T(8,128)} custom-call(f32[864,256]{1,0:T(8,128)} %wave_ref.1, f32[4,343,343]{2,1,0:T(8,128)} %copy.5.ops_ref, s32[4,343]{1,0:T(4,128)} %map_ref.1, s32[1,144]{1,0:T(1,128)} %bitcast.1), custom_call_target="tpu_custom_call" | custom-call | tf_op jit(solution)/shard_map/filtered_bands/pallas_call | solution.py:476
  64.5 2.1 %copy.7 = f32[864,256]{1,0:T(8,128)} copy(f32[864,256]{1,0:T(8,128)} %filtered_bands.1) | data formatting | bytes 1769472

commit v4 on v3

--- a/solution.py
+++ b/solution.py
@@ -90,11 +90,8 @@
     def merged(wide):
         return wide[:, :W] + wide[:, W:]
 
-    def ops_copy(c):
-        return pltpu.make_async_copy(ops_ref.at[c], w.ops.at[c], w.ops_sem.at[c])
-
-    for c in range(C):
-        ops_copy(c).start()
+    ops_copy = pltpu.make_async_copy(ops_ref, w.ops, w.ops_sem)
+    ops_copy.start()
 
     w.index[...] = jnp.full(w.index.shape, -1.0, f32)
     w.index[pl.ds(0, C), pl.ds(0, s.nodes)] = map_ref[...].astype(f32)
@@ -142,8 +139,9 @@
         row = w.index[c : c + 1, :]
         w.put_own[:, pl.ds(c * L, L)] = one_hot(row == iota((s.own, L), 0))
         w.put_face[:, pl.ds(c * L, L)] = one_hot(row - float(s.own) == iota((s.face, L), 0))
-        ops_copy(c).wait()
-        w.op_pad[c, pl.ds(0, s.nodes), pl.ds(0, s.nodes)] = w.ops[c]
+        if c == 0:
+            ops_copy.wait()
+        w.op_pad[c, pl.ds(0, s.nodes), pl.ds(0, s.nodes)] = w.ops[:, c, :]
         high, low = halves(w.op_pad[c])
         w.op_high[c] = high
         w.op_low[c] = low
@@ -410,8 +408,8 @@
         put_own=V((s.own, C * L), bf16),
         put_face=V((s.face, C * L), bf16),
         put_back=V((s.own, s.face_pad), bf16),
-        ops=V((C, s.nodes, s.nodes), f32),
-        ops_sem=dma((C,)),
+        ops=V((s.nodes, C, s.nodes), f32),
+        ops_sem=dma,
         op_pad=V((C, R, L), f32),
         op_high=V((C, R, L), bf16),
         op_low=V((C, R, L), bf16),
@@ -482,7 +480,7 @@
         compiler_params=pltpu.CompilerParams(
             collective_id=0, has_side_effects=True, vmem_limit_bytes=60 * 1024 * 1024),
         name="filtered_bands",
-    )(wavefun, cell_ops, cell_map, face_list.reshape(1, -1))
+    )(wavefun, jnp.swapaxes(cell_ops, 0, 1), cell_map, face_list.reshape(1, -1))
     if s.gram:
         return latest
     full_bands = lax.all_gather(latest, "band", axis=1, tiled=True)

time: 66.9 us -> 63.7 us (0.952)
  local copies, waits for them, and re-layouts: 5.22 us -> 2.14 us
    unnamed x2 -> x1, local copies, waits for them, and re-layouts: 5.22 us -> 2.14 us
where the time goes in v4:
time: 63.7 us; the launch traced here: 63.6 us
  Pallas kernels  61.4 us (96%)
  local copies, waits for them, and re-layouts  2.14 us (3%)
    pallas_call x1, Pallas kernels, on_device(): pl.pallas_call(functools.partial(kernel, s, list(scratch)), out_shape=jax...  61.4 us
    unnamed x1, local copies, waits for them, and re-layouts  2.14 us

profile of v4, /device:TPU:0, one launch (start us, length us, event | category | flops | bytes accessed | tf_op | source)
XLA Modules:
  0.0 63.6 jit_solution(9372383481689751479)
XLA Ops:
  0.0 61.4 %filtered_bands.1 = f32[864,256]{1,0:T(8,128)} custom-call(f32[864,256]{1,0:T(8,128)} %wave_ref.1, f32[343,4,343]{2,1,0:T(4,128)} %bitcast.2, s32[4,343]{1,0:T(4,128)} %map_ref.1, s32[1,144]{1,0:T(1,128)} %bitcast.3), custom_call_target="tpu_custom_call" | custom-call | tf_op jit(solution)/shard_map/filtered_bands/pallas_call | solution.py:474
  61.4 2.1 %copy.6 = f32[864,256]{1,0:T(8,128)} copy(f32[864,256]{1,0:T(8,128)} %filtered_bands.1) | data formatting | bytes 1769472
